TPU v7x, 32 devices: a whole 2x2x4 slice. The times are simulated.
32 devices in a mesh: prow: 4 (over y, x), pcol: 8 (over z, core).
Axes of the slice: x: 2, y: 2, z: 4, core: 2. Of those that a mesh axis runs over, the one named last changes fastest.
Arguments:
- rhs: bfloat16 [3, 8, 512, 128], P(None, 'pcol', 'prow'), may hold values from -6 to 6
- inverse_diagonal_blocks: bfloat16 [3, 8, 512, 512], P(None, 'pcol'), may hold values from -1 to 2, as said below
- offdiagonal_blocks: bfloat16 [2, 8, 4, 512, 512], P(None, 'pcol', 'prow'), may hold values from -0.09375 to 0.09375
- targets: int32 [2, 8, 4], P(None, 'pcol'), may hold values from 0 to 15, as said below
Outputs:
- solution: bfloat16 [3, 8, 512, 128], P(None, 'pcol', 'prow')
Inputs may be any that keep to these rules, and one draw needn't show every extreme that they name: For a supernode of level l the 4 entries of targets[l] are distinct and lie between l * 8 and (2) * 8 - 1, so they name supernodes of later levels only. Each block of inverse_diagonal_blocks is lower triangular.
All inputs are finite; a program needn't handle non-finite values.
Results may differ from a plain program's by a relative error of at most 0.014.
Values may be sent and summed in bfloat16 or wider, within the bound.
No kernel may reach another device: no remote copies, remote signals or barrier semaphores. Data moves between devices by JAX's collectives and lax.ppermute only.
A program may use at most 64 MiB of HBM per device.

v0:
```python
import jax
import jax.numpy as jnp
from jax import lax
from jax.sharding import PartitionSpec as P


def local(rhs, inverse_diagonal_blocks, offdiagonal_blocks, targets):
    levels = rhs.shape[0]
    per_group = rhs.shape[1]
    part_rows = rhs.shape[2]
    vector_count = rhs.shape[3]
    per_device = offdiagonal_blocks.shape[2]
    row_count = lax.axis_size("prow")
    level_size = per_group * lax.axis_size("pcol")
    upper_count = levels - 1
    row_index = lax.axis_index("prow")
    gathered_updates = jnp.zeros(
        (upper_count, row_count, level_size, part_rows, vector_count), jnp.float32
    )
    outputs = []
    for present_level in range(levels):
        remaining_rhs = rhs[present_level].astype(jnp.float32)
        if present_level > 0:
            due_block = gathered_updates[present_level - 1]
            reduced_once = lax.psum_scatter(
                due_block.astype(jnp.bfloat16), "pcol", scatter_dimension=1, tiled=True
            )
            arrived = lax.psum_scatter(
                reduced_once, "prow", scatter_dimension=0, tiled=True
            ).astype(jnp.float32)[0]
            remaining_rhs = remaining_rhs - arrived
        whole_block = lax.all_gather(remaining_rhs, "prow", axis=1, tiled=True)
        finished_unknowns = jnp.einsum(
            "rqe,rei->rqi",
            inverse_diagonal_blocks[present_level].astype(jnp.float32),
            whole_block,
            precision=lax.Precision.HIGHEST,
        ).astype(jnp.bfloat16)
        supernode_rows = lax.dynamic_slice_in_dim(
            finished_unknowns, row_index * part_rows, part_rows, 1
        )
        outputs.append(supernode_rows)
        if present_level < upper_count:
            products = jnp.einsum(
                "wsiq,wqm->wsim",
                offdiagonal_blocks[present_level],
                finished_unknowns,
                preferred_element_type=jnp.float32,
            )
            chosen = lax.dynamic_slice_in_dim(
                targets[present_level], row_index * per_device, per_device, 1
            )
            chosen = chosen.reshape(per_group * per_device)
            level_ids = chosen // level_size
            node_ids = chosen % level_size
            moved_rows = products.reshape(
                per_group * per_device, row_count, part_rows, vector_count
            )
            gathered_updates = gathered_updates.at[level_ids, :, node_ids].add(moved_rows)
    return jnp.stack(outputs)


def solution(mesh):
    in_specs = (
        P(None, "pcol", "prow", None),
        P(None, "pcol", None, None),
        P(None, "pcol", "prow", None, None),
        P(None, "pcol", None),
    )
    out_specs = P(None, "pcol", "prow", None)
    return jax.shard_map(local, mesh=mesh, in_specs=in_specs, out_specs=out_specs, check_vma=False)
```

profile of v0, /device:TPU:0, one launch (start us, length us, event | category | flops | bytes accessed | tf_op | source)
XLA Modules:
  0.0 184.7 jit_solution(10603757281627997184)
XLA Ops:
  6.5 0.0 reduce-scatter.15.cloned.1.call-start
  6.5 0.7 fusion.22
  7.2 0.6 constant_dynamic-slice_fusion
  13.0 0.8 fusion.21
  13.8 10.5 %all-gather = f32[1,1,512,128]{3,2,1,0:T(8,128)S(1)} all-gather(f32[1,1,128,128]{3,2,1,0:T(8,128)S(1)} %get-tuple-element.35), channel_id=2, replica_groups=mesh['prow'=4,'pcol'=8] {'prow'}, dimensions={2}, use_global_device_ids=true | all-gather | bytes 327680 | tf_op jit(solution)/shard_map/all_gather | solution.py:32
  24.3 1.3 fusion.20
  25.6 0.1 concatenate.10
  25.7 0.1 concatenate.11
  25.7 1.6 convolution_convert_fusion.1
  27.4 1.4 and_reduce_fusion
  28.7 0.0 copy-start.1
  28.7 0.5 broadcast_in_dim.2
  29.2 0.9 fusion.1
  30.2 0.0 copy-start
  30.2 1.9 %copy-done = f32[2,4,8,128,128]{3,4,1,2,0:T(8,128)} copy-done((f32[2,4,8,128,128]{3,4,1,2,0:T(8,128)}, f32[2,4,8,128,128]{3,4,1,2,0:T(8,128)S(1)}, u32[]{:S(2)}) %copy-start) | copy-done | bytes 4194328
  32.1 1.1 fusion.5
  33.3 0.0 reduce-scatter.15.cloned.1.call-update
  33.3 0.0 reduce-scatter.19.cloned.1.call-start
  33.3 33.0 %reduce-scatter.15.cloned.1.call-done = bf16[4,1,128,128]{2,3,0,1:T(8,128)(2,1)} async-done(((bf16[4,8,128,128]{2,3,0,1:T(8,128)(2,1)}), bf16[4,1,128,128]{2,3,0,1:T(8,128)(2,1)}) %reduce-scatter.15.cloned.1.call-update) | async-done | bytes 131088 | tf_op jit(solution)/shard_map/reduce_scatter | solution.py:25
  66.3 0.0 reduce-scatter.19.cloned.1.call-update
  66.4 0.0 reduce-scatter.17.cloned.1.call-start
  66.4 0.1 copy.25
  66.5 24.9 %reduce-scatter.19.cloned.1.call-done = bf16[1,1,128,128]{2,3,0,1:T(8,128)(2,1)} async-done(((bf16[4,1,128,128]{2,3,0,1:T(8,128)(2,1)}), bf16[1,1,128,128]{2,3,0,1:T(8,128)(2,1)}) %reduce-scatter.19.cloned.1.call-update) | async-done | bytes 32784
  91.4 0.8 convert_subtract_fusion.1
  92.2 10.0 %all-gather.1 = f32[1,1,512,128]{2,3,0,1:T(8,128)S(1)} all-gather(f32[1,1,128,128]{2,3,0,1:T(8,128)S(1)} %convert_subtract_fusion.1), channel_id=3, replica_groups=mesh['prow'=4,'pcol'=8] {'prow'}, dimensions={2}, use_global_device_ids=true | all-gather | bytes 327680 | tf_op jit(solution)/shard_map/all_gather | solution.py:32
  102.2 0.0 copy-done.1
  102.2 0.7 convolution_convert_fusion
  102.9 2.6 %fusion.4 = f32[2,4,8,128,128]{3,4,1,2,0:T(8,128)} fusion(f32[2,4,8,128,128]{3,4,1,2,0:T(8,128)} %copy-done, s32[]{:T(128)} %bitcast.16, s32[]{:T(128)} %bitcast.17, bf16[4,128,512]{2,1,0:T(8,128)(2,1)S(1)} %bitcast.81, bf16[128,512]{1,0:T(8,128)(2,1)S(1)} %convolution_convert_fusion, pred[]{:T(512)} %get-tuple-element.29), kind=kOutput, calls=%fused_computation.8 | convolution fusion | flops 67239936 | bytes 1181184 | tf_op jit(solution)/shard_map/wsiq,wqm->wsim/dot_general | solution.py:44
  105.5 2.7 %fusion.6 = bf16[4,8,128,128]{2,3,0,1:T(8,128)(2,1)} fusion(f32[2,4,8,128,128]{3,4,1,2,0:T(8,128)} %fusion.4), kind=kLoop, calls=%fused_computation.12 | loop fusion | bytes 2097152 | tf_op jit(solution)/shard_map/convert_element_type | solution.py:26
  108.2 0.0 reduce-scatter.17.cloned.1.call-update
  108.2 0.0 reduce-scatter.21.cloned.1.call-start
  108.2 32.7 %reduce-scatter.17.cloned.1.call-done = bf16[4,1,128,128]{2,3,0,1:T(8,128)(2,1)} async-done(((bf16[4,8,128,128]{2,3,0,1:T(8,128)(2,1)}), bf16[4,1,128,128]{2,3,0,1:T(8,128)(2,1)}) %reduce-scatter.17.cloned.1.call-update) | async-done | bytes 131088 | tf_op jit(solution)/shard_map/reduce_scatter | solution.py:25
  140.9 0.0 reduce-scatter.21.cloned.1.call-update
  141.0 0.1 copy.26
  141.1 0.1 copy.17
  141.2 24.6 %reduce-scatter.21.cloned.1.call-done = bf16[1,1,128,128]{2,3,0,1:T(8,128)(2,1)} async-done(((bf16[4,1,128,128]{2,3,0,1:T(8,128)(2,1)}), bf16[1,1,128,128]{2,3,0,1:T(8,128)(2,1)}) %reduce-scatter.21.cloned.1.call-update) | async-done | bytes 32784
  165.9 0.8 convert_subtract_fusion
  166.7 10.0 %all-gather.2 = f32[1,1,512,128]{2,3,0,1:T(8,128)S(1)} all-gather(f32[1,1,128,128]{2,3,0,1:T(8,128)S(1)} %convert_subtract_fusion), channel_id=4, replica_groups=mesh['prow'=4,'pcol'=8] {'prow'}, dimensions={2}, use_global_device_ids=true | all-gather | bytes 327680 | tf_op jit(solution)/shard_map/all_gather | solution.py:32
  176.7 0.7 fusion.7
  177.4 0.8 copy.18
  (4 shorter events, 0.1 us)
Async XLA Ops:
  6.5 59.8 %reduce-scatter.15.cloned.1.call-start = ((), (), s32[]{:S(2)}) async-start(), calls=%async_computation.4 | async-start | bytes 1179648 | tf_op jit(solution)/shard_map/reduce_scatter | solution.py:25
  28.7 73.4 %copy-start.1 = (bf16[3,1,512,512]{3,2,1,0:T(8,128)(2,1)S(1)}, bf16[3,1,512,512]{3,2,1,0:T(8,128)(2,1)}, u32[]{:S(2)}) copy-start(bf16[3,1,512,512]{3,2,1,0:T(8,128)(2,1)} %param.9) | copy-start | bytes 4718596
  30.2 1.9 %copy-start = (f32[2,4,8,128,128]{3,4,1,2,0:T(8,128)}, f32[2,4,8,128,128]{3,4,1,2,0:T(8,128)S(1)}, u32[]{:S(2)}) copy-start(f32[2,4,8,128,128]{3,4,1,2,0:T(8,128)S(1)} %fusion.1) | copy-start | bytes 12582916
  33.3 58.1 %reduce-scatter.19.cloned.1.call-start = ((), (), s32[]{:S(2)}) async-start(), calls=%async_computation.6 | async-start | bytes 163840
  66.4 74.6 %reduce-scatter.17.cloned.1.call-start = ((), (), s32[]{:S(2)}) async-start(), calls=%async_computation.5 | async-start | bytes 1179648 | tf_op jit(solution)/shard_map/reduce_scatter | solution.py:25
  108.2 57.7 %reduce-scatter.21.cloned.1.call-start = ((), (), s32[]{:S(2)}) async-start(), calls=%async_computation.7 | async-start | bytes 163840
Sparse Core Ops, SparseCore 0:
  33.4 32.8 reduce-scatter.14
  69.1 22.3 reduce-scatter.18
  108.3 32.5 reduce-scatter.16
  143.5 22.3 reduce-scatter.20
where the time goes:
time: 185 us
  waiting for transfers between devices  115 us (62%)
  blocking collectives  30.4 us (16%)
  between operations  18.4 us (10%)
  local copies, waits for them, and re-layouts  10.1 us (5%)
  matrix products  6.49 us (4%)
  other arithmetic  3.72 us (2%)
    reduce_scatter x2, waiting for transfers between devices, local(): lax.psum_scatter(due_block.astype(jnp.bfloat16), 'pcol', scatter_dimensio...  65.7 us
    unnamed x6, waiting for transfers between devices  49.6 us
    all_gather x3, blocking collectives, local(): whole_block = lax.all_gather(remaining_rhs, 'prow', axis=1, tiled=True)  30.4 us
    convert_element_type x2, local copies, waits for them, and re-layouts, local(): due_block.astype(jnp.bfloat16)  3.85 us
  transfers between devices with their start and end apart: 4, of which 4 were waited for; matrix products, arithmetic and copies ran while one was open for 0% of the time, Pallas kernels for 0%

commit v1 on v0

--- a/solution.py
+++ b/solution.py
@@ -29,7 +29,29 @@
                 reduced_once, "prow", scatter_dimension=0, tiled=True
             ).astype(jnp.float32)[0]
             remaining_rhs = remaining_rhs - arrived
-        whole_block = lax.all_gather(remaining_rhs, "prow", axis=1, tiled=True)
+        inbox = []
+        axis_total = lax.axis_size("prow")
+        hop_no = 0
+        while hop_no < axis_total:
+            inbox.append((hop_no, (hop_no + 1) % axis_total))
+            hop_no += 1
+        hop_no = 0
+        buffer = []
+        while hop_no < axis_total:
+            buffer.append((hop_no, (hop_no - 1) % axis_total))
+            hop_no += 1
+        upper, m_next = ([remaining_rhs], [remaining_rhs])
+        for _ in range(axis_total // 2):
+            upper.append(lax.ppermute(upper[-1], "prow", inbox))
+        src_i = 0
+        while src_i < (axis_total - 1) // 2:
+            m_next.append(lax.ppermute(m_next[-1], "prow", buffer))
+            src_i = src_i + 1
+        whole_block = jnp.roll(
+            jnp.concatenate([*upper[::-1], *m_next[1:]], axis=1),
+            (lax.axis_index("prow") - axis_total // 2) * remaining_rhs.shape[1],
+            axis=1,
+        )
         finished_unknowns = jnp.einsum(
             "rqe,rei->rqi",
             inverse_diagonal_blocks[present_level].astype(jnp.float32),

time: 185 us -> 184 us (level)
  blocking collectives: 30.4 us -> 0 us
  waiting for transfers between devices: 115 us -> 132 us
  starting transfers between devices: 0.12 us -> 12.6 us
    all_gather x3 -> x0, blocking collectives: 30.4 us -> none  [local(): whole_block = lax.all_gather(remaining_rhs, 'prow', axis=1, tiled=True)]
    ppermute x0 -> x9, waiting for transfers between devices: none -> 16.1 us  [the longest x6 16.1 us: local(): upper.append(lax.ppermute(upper[-1], 'prow', inbox))]
    ppermute x0 -> x9, starting transfers between devices: none -> 12.5 us  [the longest x6 8.56 us: local(): upper.append(lax.ppermute(upper[-1], 'prow', inbox))]
  transfers between devices with their start and end apart: 4 -> 13, of which waited for: 4 -> 9; matrix products, arithmetic and copies ran while one was open for 0% -> 2% of each run, Pallas kernels for 0% -> 0%
where the time goes in v1:
time: 184 us
  waiting for transfers between devices  132 us (72%)
  between operations  18.4 us (10%)
  starting transfers between devices  12.6 us (7%)
  local copies, waits for them, and re-layouts  10 us (5%)
  matrix products  6.93 us (4%)
  other arithmetic  3.71 us (2%)
    reduce_scatter x2, waiting for transfers between devices, local(): lax.psum_scatter(due_block.astype(jnp.bfloat16), 'pcol', scatter_dimensio...  66.1 us
    unnamed x6, waiting for transfers between devices  49.9 us
    ppermute x6, waiting for transfers between devices, local(): upper.append(lax.ppermute(upper[-1], 'prow', inbox))  16.1 us
    ppermute x6, starting transfers between devices, local(): upper.append(lax.ppermute(upper[-1], 'prow', inbox))  8.56 us
    ppermute x3, starting transfers between devices, local(): m_next.append(lax.ppermute(m_next[-1], 'prow', buffer))  3.96 us
    convert_element_type x2, local copies, waits for them, and re-layouts, local(): due_block.astype(jnp.bfloat16)  3.84 us
  transfers between devices with their start and end apart: 13, of which 9 were waited for; matrix products, arithmetic and copies ran while one was open for 2% of the time, Pallas kernels for 0%

profile of v1, /device:TPU:0, one launch (start us, length us, event | category | flops | bytes accessed | tf_op | source)
XLA Modules:
  0.0 183.8 jit_solution(11204651528277809260)
XLA Ops:
  6.5 0.0 reduce-scatter.15.cloned.1.call-start
  6.5 0.8 fusion.54
  7.3 3.0 %collective-permute-start = (f32[1,128,128]{2,1,0:T(8,128)S(1)}, f32[1,128,128]{2,1,0:T(8,128)S(1)}, u32[]{:S(2)}, u32[]{:S(2)}) collective-permute-start(f32[1,128,128]{2,1,0:T(8,128)S(1)} %get-tuple-element.36), channel_id=1, source_target_pairs={{0,8},{8,16},{16,24},{24,0},{1,9},{9,17},{17,25},{25,1},{2,10},{10... | collective-permute-start | bytes 196616 | tf_op jit(solution)/shard_map/ppermute | solution.py:45
  10.4 1.0 collective-permute-start.2
  11.4 1.3 fusion.53
  12.7 0.7 fusion.55
  13.3 0.6 constant_dynamic-slice_fusion
  19.1 0.1 concatenate.23
  19.2 0.1 concatenate.25
  19.3 0.0 collective-permute-done
  19.3 1.0 collective-permute-start.1
  20.3 1.4 and_reduce_fusion
  21.7 0.0 collective-permute-done.2
  21.7 2.8 %collective-permute-done.1 = f32[1,128,128]{2,1,0:T(8,128)S(1)} collective-permute-done((f32[1,128,128]{2,1,0:T(8,128)S(1)}, f32[1,128,128]{2,1,0:T(8,128)S(1)}, u32[]{:S(2)}, u32[]{:S(2)}) %collective-permute-start.1) | collective-permute-done | bytes 65568 | tf_op jit(solution)/shard_map/ppermute | solution.py:45
  24.5 2.2 %convolution_convert_fusion.1 = bf16[128,512]{1,0:T(8,128)(2,1)S(1)} fusion(bf16[3,1,512,512]{3,2,1,0:T(8,128)(2,1)} %param.11, s32[]{:T(128)S(6)} %select_n.64, f32[1,128,128]{2,1,0:T(8,128)S(1)} %collective-permute-done.1, f32[1,128,128]{2,1,0:T(8,128)S(1)} %collective-permute-done, f32[1,128,128]{2,1,0:T(8,128)S(1)} %get-tuple-element.36, ...), kind=kOutput, calls=%fused_computation.10 | convolution fusion | flops 403177472 | bytes 917508 | tf_op jit(solution)/shard_map/rqe,rei->rqi/dot_general | solution.py:55
  26.7 0.0 copy-start.1
  26.7 0.5 broadcast_in_dim.2
  27.2 0.9 fusion.1
  28.2 0.0 copy-start
  28.2 1.9 %copy-done = f32[2,4,8,128,128]{3,4,1,2,0:T(8,128)} copy-done((f32[2,4,8,128,128]{3,4,1,2,0:T(8,128)}, f32[2,4,8,128,128]{3,4,1,2,0:T(8,128)S(1)}, u32[]{:S(2)}) %copy-start) | copy-done | bytes 4194328
  30.1 1.1 fusion.5
  31.2 0.0 reduce-scatter.15.cloned.1.call-update
  31.3 0.0 reduce-scatter.19.cloned.1.call-start
  31.3 33.4 %reduce-scatter.15.cloned.1.call-done = bf16[4,1,128,128]{2,3,0,1:T(8,128)(2,1)} async-done(((bf16[4,8,128,128]{2,3,0,1:T(8,128)(2,1)}), bf16[4,1,128,128]{2,3,0,1:T(8,128)(2,1)}) %reduce-scatter.15.cloned.1.call-update) | async-done | bytes 131088 | tf_op jit(solution)/shard_map/reduce_scatter | solution.py:25
  64.7 0.0 reduce-scatter.19.cloned.1.call-update
  64.7 0.0 reduce-scatter.17.cloned.1.call-start
  64.8 0.1 copy.15
  64.9 25.0 %reduce-scatter.19.cloned.1.call-done = bf16[1,1,128,128]{2,3,0,1:T(8,128)(2,1)} async-done(((bf16[4,1,128,128]{2,3,0,1:T(8,128)(2,1)}), bf16[1,1,128,128]{2,3,0,1:T(8,128)(2,1)}) %reduce-scatter.19.cloned.1.call-update) | async-done | bytes 32784
  89.9 0.8 subtract_bitcast_fusion.1
  90.7 1.5 collective-permute-start.3
  92.2 1.5 collective-permute-start.5
  93.6 2.2 %collective-permute-done.3 = f32[1,128,128]{1,2,0:T(8,128)S(1)} collective-permute-done((f32[1,128,128]{1,2,0:T(8,128)S(1)}, f32[1,128,128]{1,2,0:T(8,128)S(1)}, u32[]{:S(2)}, u32[]{:S(2)}) %collective-permute-start.3) | collective-permute-done | bytes 65568 | tf_op jit(solution)/shard_map/ppermute | solution.py:45
  95.9 0.8 collective-permute-start.4
  96.6 0.0 collective-permute-done.5
  96.6 4.4 %collective-permute-done.4 = f32[1,128,128]{1,2,0:T(8,128)S(1)} collective-permute-done((f32[1,128,128]{1,2,0:T(8,128)S(1)}, f32[1,128,128]{1,2,0:T(8,128)S(1)}, u32[]{:S(2)}, u32[]{:S(2)}) %collective-permute-start.4) | collective-permute-done | bytes 65568 | tf_op jit(solution)/shard_map/ppermute | solution.py:45
  101.0 0.0 copy-done.1
  101.0 0.6 convolution_convert_fusion
  101.7 2.5 %fusion.4 = f32[2,4,8,128,128]{3,4,1,2,0:T(8,128)} fusion(f32[2,4,8,128,128]{3,4,1,2,0:T(8,128)} %copy-done, s32[]{:T(128)} %bitcast.20, s32[]{:T(128)} %bitcast.21, bf16[4,128,512]{2,1,0:T(8,128)(2,1)S(1)} %bitcast.90, bf16[128,512]{1,0:T(8,128)(2,1)S(1)} %convolution_convert_fusion, pred[]{:T(512)} %get-tuple-element.30), kind=kOutput, calls=%fused_computation.8 | convolution fusion | flops 67239936 | bytes 1181184 | tf_op jit(solution)/shard_map/wsiq,wqm->wsim/dot_general | solution.py:66
  104.2 2.7 %fusion.6 = bf16[4,8,128,128]{2,3,0,1:T(8,128)(2,1)} fusion(f32[2,4,8,128,128]{3,4,1,2,0:T(8,128)} %fusion.4), kind=kLoop, calls=%fused_computation.12 | loop fusion | bytes 2097152 | tf_op jit(solution)/shard_map/convert_element_type | solution.py:26
  106.9 0.0 reduce-scatter.17.cloned.1.call-update
  106.9 0.0 reduce-scatter.21.cloned.1.call-start
  107.0 32.7 %reduce-scatter.17.cloned.1.call-done = bf16[4,1,128,128]{2,3,0,1:T(8,128)(2,1)} async-done(((bf16[4,8,128,128]{2,3,0,1:T(8,128)(2,1)}), bf16[4,1,128,128]{2,3,0,1:T(8,128)(2,1)}) %reduce-scatter.17.cloned.1.call-update) | async-done | bytes 131088 | tf_op jit(solution)/shard_map/reduce_scatter | solution.py:25
  139.7 0.0 reduce-scatter.21.cloned.1.call-update
  139.7 0.1 copy.16
  139.8 24.9 %reduce-scatter.21.cloned.1.call-done = bf16[1,1,128,128]{2,3,0,1:T(8,128)(2,1)} async-done(((bf16[4,1,128,128]{2,3,0,1:T(8,128)(2,1)}), bf16[1,1,128,128]{2,3,0,1:T(8,128)(2,1)}) %reduce-scatter.21.cloned.1.call-update) | async-done | bytes 32784
  164.7 0.8 subtract_bitcast_fusion
  165.4 1.5 collective-permute-start.6
  166.9 1.5 collective-permute-start.8
  168.4 2.2 %collective-permute-done.6 = f32[1,128,128]{1,2,0:T(8,128)S(1)} collective-permute-done((f32[1,128,128]{1,2,0:T(8,128)S(1)}, f32[1,128,128]{1,2,0:T(8,128)S(1)}, u32[]{:S(2)}, u32[]{:S(2)}) %collective-permute-start.6) | collective-permute-done | bytes 65568 | tf_op jit(solution)/shard_map/ppermute | solution.py:45
  170.6 0.8 collective-permute-start.7
  171.4 0.0 collective-permute-done.8
  171.4 4.4 %collective-permute-done.7 = f32[1,128,128]{1,2,0:T(8,128)S(1)} collective-permute-done((f32[1,128,128]{1,2,0:T(8,128)S(1)}, f32[1,128,128]{1,2,0:T(8,128)S(1)}, u32[]{:S(2)}, u32[]{:S(2)}) %collective-permute-start.7) | collective-permute-done | bytes 65568 | tf_op jit(solution)/shard_map/ppermute | solution.py:45
  175.8 0.6 fusion.7
  176.5 0.8 copy.10
  (4 shorter events, 0.0 us)
Async XLA Ops:
  6.5 58.2 %reduce-scatter.15.cloned.1.call-start = ((), (), s32[]{:S(2)}) async-start(), calls=%async_computation.4 | async-start | bytes 1179648 | tf_op jit(solution)/shard_map/reduce_scatter | solution.py:25
  7.3 12.0 %collective-permute-start = (f32[1,128,128]{2,1,0:T(8,128)S(1)}, f32[1,128,128]{2,1,0:T(8,128)S(1)}, u32[]{:S(2)}, u32[]{:S(2)}) collective-permute-start(f32[1,128,128]{2,1,0:T(8,128)S(1)} %get-tuple-element.36), channel_id=1, source_target_pairs={{0,8},{8,16},{16,24},{24,0},{1,9},{9,17},{17,25},{25,1},{2,10},{10... | collective-permute-start | bytes 196616 | tf_op jit(solution)/shard_map/ppermute | solution.py:45
  10.4 11.3 %collective-permute-start.2 = (f32[1,128,128]{2,1,0:T(8,128)S(1)}, f32[1,128,128]{2,1,0:T(8,128)S(1)}, u32[]{:S(2)}, u32[]{:S(2)}) collective-permute-start(f32[1,128,128]{2,1,0:T(8,128)S(1)} %get-tuple-element.36), channel_id=1, source_target_pairs={{0,24},{8,0},{16,8},{24,16},{1,25},{9,1},{17,9},{25,17},{2,26},{10... | collective-permute-start | bytes 196616 | tf_op jit(solution)/shard_map/ppermute | solution.py:48
  19.3 5.2 %collective-permute-start.1 = (f32[1,128,128]{2,1,0:T(8,128)S(1)}, f32[1,128,128]{2,1,0:T(8,128)S(1)}, u32[]{:S(2)}, u32[]{:S(2)}) collective-permute-start(f32[1,128,128]{2,1,0:T(8,128)S(1)} %collective-permute-done), channel_id=1, source_target_pairs={{0,8},{8,16},{16,24},{24,0},{1,9},{9,17},{17,25},{25,1},{2,10},{10... | collective-permute-start | bytes 196616 | tf_op jit(solution)/shard_map/ppermute | solution.py:45
  26.7 74.3 %copy-start.1 = (bf16[3,1,512,512]{3,2,1,0:T(8,128)(2,1)S(1)}, bf16[3,1,512,512]{3,2,1,0:T(8,128)(2,1)}, u32[]{:S(2)}) copy-start(bf16[3,1,512,512]{3,2,1,0:T(8,128)(2,1)} %param.11) | copy-start | bytes 4718596
  28.2 1.9 %copy-start = (f32[2,4,8,128,128]{3,4,1,2,0:T(8,128)}, f32[2,4,8,128,128]{3,4,1,2,0:T(8,128)S(1)}, u32[]{:S(2)}) copy-start(f32[2,4,8,128,128]{3,4,1,2,0:T(8,128)S(1)} %fusion.1) | copy-start | bytes 12582916
  31.3 58.6 %reduce-scatter.19.cloned.1.call-start = ((), (), s32[]{:S(2)}) async-start(), calls=%async_computation.6 | async-start | bytes 163840
  64.7 74.9 %reduce-scatter.17.cloned.1.call-start = ((), (), s32[]{:S(2)}) async-start(), calls=%async_computation.5 | async-start | bytes 1179648 | tf_op jit(solution)/shard_map/reduce_scatter | solution.py:25
  90.7 5.2 %collective-permute-start.3 = (f32[1,128,128]{1,2,0:T(8,128)S(1)}, f32[1,128,128]{1,2,0:T(8,128)S(1)}, u32[]{:S(2)}, u32[]{:S(2)}) collective-permute-start(f32[1,128,128]{1,2,0:T(8,128)S(1)} %subtract_bitcast_fusion.1), channel_id=1, source_target_pairs={{0,8},{8,16},{16,24},{24,0},{1,9},{9,17},{17,25},{25,1},{2,10},{10... | collective-permute-start | bytes 196616 | tf_op jit(solution)/shard_map/ppermute | solution.py:45
  92.2 4.5 %collective-permute-start.5 = (f32[1,128,128]{1,2,0:T(8,128)S(1)}, f32[1,128,128]{1,2,0:T(8,128)S(1)}, u32[]{:S(2)}, u32[]{:S(2)}) collective-permute-start(f32[1,128,128]{1,2,0:T(8,128)S(1)} %subtract_bitcast_fusion.1), channel_id=1, source_target_pairs={{0,24},{8,0},{16,8},{24,16},{1,25},{9,1},{17,9},{25,17},{2,26},{10... | collective-permute-start | bytes 196616 | tf_op jit(solution)/shard_map/ppermute | solution.py:48
  95.9 5.2 %collective-permute-start.4 = (f32[1,128,128]{1,2,0:T(8,128)S(1)}, f32[1,128,128]{1,2,0:T(8,128)S(1)}, u32[]{:S(2)}, u32[]{:S(2)}) collective-permute-start(f32[1,128,128]{1,2,0:T(8,128)S(1)} %collective-permute-done.3), channel_id=1, source_target_pairs={{0,8},{8,16},{16,24},{24,0},{1,9},{9,17},{17,25},{25,1},{2,10},{10... | collective-permute-start | bytes 196616 | tf_op jit(solution)/shard_map/ppermute | solution.py:45
  106.9 57.7 %reduce-scatter.21.cloned.1.call-start = ((), (), s32[]{:S(2)}) async-start(), calls=%async_computation.7 | async-start | bytes 163840
  165.4 5.2 %collective-permute-start.6 = (f32[1,128,128]{1,2,0:T(8,128)S(1)}, f32[1,128,128]{1,2,0:T(8,128)S(1)}, u32[]{:S(2)}, u32[]{:S(2)}) collective-permute-start(f32[1,128,128]{1,2,0:T(8,128)S(1)} %subtract_bitcast_fusion), channel_id=1, source_target_pairs={{0,8},{8,16},{16,24},{24,0},{1,9},{9,17},{17,25},{25,1},{2,10},{10... | collective-permute-start | bytes 196616 | tf_op jit(solution)/shard_map/ppermute | solution.py:45
  166.9 4.5 %collective-permute-start.8 = (f32[1,128,128]{1,2,0:T(8,128)S(1)}, f32[1,128,128]{1,2,0:T(8,128)S(1)}, u32[]{:S(2)}, u32[]{:S(2)}) collective-permute-start(f32[1,128,128]{1,2,0:T(8,128)S(1)} %subtract_bitcast_fusion), channel_id=1, source_target_pairs={{0,24},{8,0},{16,8},{24,16},{1,25},{9,1},{17,9},{25,17},{2,26},{10... | collective-permute-start | bytes 196616 | tf_op jit(solution)/shard_map/ppermute | solution.py:48
  170.6 5.2 %collective-permute-start.7 = (f32[1,128,128]{1,2,0:T(8,128)S(1)}, f32[1,128,128]{1,2,0:T(8,128)S(1)}, u32[]{:S(2)}, u32[]{:S(2)}) collective-permute-start(f32[1,128,128]{1,2,0:T(8,128)S(1)} %collective-permute-done.6), channel_id=1, source_target_pairs={{0,8},{8,16},{16,24},{24,0},{1,9},{9,17},{17,25},{25,1},{2,10},{10... | collective-permute-start | bytes 196616 | tf_op jit(solution)/shard_map/ppermute | solution.py:45
Sparse Core Ops, SparseCore 0:
  31.4 33.2 reduce-scatter.14
  67.4 22.3 reduce-scatter.18
  107.1 32.5 reduce-scatter.16
  142.3 22.3 reduce-scatter.20
